TPU v7x, 512 devices: a whole 4x4x16 slice. The times are simulated.
512 devices in a mesh: expert: 64 (over z, x), tensor: 8 (over y, core).
Axes of the slice: x: 4, y: 4, z: 16, core: 2. Of those that a mesh axis runs over, the one named last changes fastest.
Arguments:
- tokens: bfloat16 [8192, 7168], P('expert', 'tensor'), may hold values from -6 to 6
- route_ids: int32 [8192, 8], P('expert'), may hold values from 0 to 255, as said below
- route_weight: float32 [8192, 8], P('expert'), may hold values from 0.1 to 2.5
- gate_up: bfloat16 [64, 2, 7168, 1024], P('expert', None, None, 'tensor'), may hold values from -0.0625 to 0.0625
- block_keep: int32 [64, 2, 112, 16], P('expert', None, None, 'tensor'), may hold values 0 or 1
Outputs:
- hidden_slots: bfloat16 [64, 512, 1024], P('expert', None, 'tensor')
Inputs may be any that keep to these rules, and one draw needn't show every extreme that they name: `route_ids`: each row names 8 different experts. Within each aligned block of 128 rows no expert is named by more than 8 rows, and one expert numbered below 64 is named by exactly 8 rows in every block.
All inputs are finite; a program needn't handle non-finite values. No bound on the sum of `block_keep` on one device may be relied on, other than what follows from the above.
Results may differ from a plain program's by a relative error of at most 0.0051.
Values may be sent and summed in bfloat16 or wider, within the bound.
A program may use at most 64 MiB of HBM per device.

v0:
```python
import jax
import jax.numpy as jnp
from jax import lax
from jax.sharding import PartitionSpec as P

BLOCK = 64
CAP = 8


def expand_mask(keep_mask, block_size):
    widened = jnp.repeat(keep_mask, block_size, axis=1)
    return jnp.repeat(widened, block_size, axis=2)


def slot_table(picked, rounded, flight, capacity):
    token_count, pick_count = picked.shape
    flattened = picked.reshape(-1)
    matches = (flattened[:, None] == jnp.arange(flight, dtype=jnp.int32)[None, :]).astype(jnp.int32)
    before = jnp.cumsum(matches, axis=0) - matches
    slot_rank = jnp.sum(before * matches, axis=1)
    in_window = flattened < flight
    target = jnp.where(in_window, flattened * capacity + slot_rank, flight * capacity)
    source_row = jnp.arange(token_count * pick_count, dtype=jnp.int32) // pick_count
    token_of = jnp.full((flight * capacity,), -1, jnp.int32).at[target].set(source_row, mode="drop")
    weight_of = (
        jnp.zeros((flight * capacity,), rounded.dtype)
        .at[target]
        .set(rounded.reshape(-1), mode="drop")
    )
    return (token_of, weight_of)


def activate(totals, scaling):
    factor = scaling.astype(jnp.float32)[..., None]
    return (factor * jax.nn.silu(totals[0]) * totals[1]).astype(jnp.bfloat16)


def shards(tokens, route_ids, route_weight, gate_up, block_keep):
    flight = lax.axis_size("expert")
    capacity = CAP
    masked = gate_up[0] * expand_mask(block_keep[0], BLOCK).astype(gate_up.dtype)
    hidden_units = masked.shape[2]
    rounded = route_weight.astype(jnp.bfloat16)
    token_of, weight_of = slot_table(route_ids, rounded, flight, capacity)
    filled = (token_of >= 0)[:, None]
    clipped = jnp.maximum(token_of, 0)
    slot_weight = weight_of.reshape(flight, capacity)
    gathered = lax.all_gather(tokens, "tensor", axis=1, tiled=True)
    picked_rows = jnp.where(
        filled, jnp.take(gathered, clipped, axis=0), jnp.zeros((), gathered.dtype)
    )
    outgoing = picked_rows.reshape(flight, capacity, gathered.shape[1])
    arrived = lax.all_to_all(outgoing, "expert", split_axis=0, concat_axis=0, tiled=True)
    scaling = lax.all_to_all(slot_weight, "expert", split_axis=0, concat_axis=0, tiled=True)
    totals = jnp.einsum("scd,kdf->kscf", arrived, masked, preferred_element_type=jnp.float32)
    hidden = activate(totals, scaling)
    hidden = hidden.reshape(1, -1, hidden_units)
    return hidden


def solution(mesh):
    return jax.shard_map(
        shards,
        mesh=mesh,
        in_specs=(
            P("expert", "tensor"),
            P("expert", None),
            P("expert", None),
            P("expert", None, None, "tensor"),
            P("expert", None, None, "tensor"),
        ),
        out_specs=P("expert", None, "tensor"),
        check_vma=False,
    )
```

profile of v0, /device:TPU:1, one launch (start us, length us, event | category | flops | bytes accessed | tf_op | source)
XLA Modules:
  0.0 435.0 jit_solution(17589274453170928703)
XLA Ops:
  6.5 0.7 all-gather.2.cloned.1.call-update
  7.3 0.8 copy.37
  8.3 18.0 %reduce-window.6 = s32[64,8,128]{2,1,0:T(8,128)S(1)} reduce-window(s32[64,8,128]{2,1,0:T(8,128)S(1)} %fusion.18, s32[]{:T(128)} %constant.46.clone.1), window={size=1x1x128 pad=0_0x0_0x127_0}, to_apply=%region_0.0 | reduce-window | flops 8323072 | bytes 524292 | tf_op jit(solution)/shard_map/reduce-window
  26.4 0.1 copy.39
  26.7 0.7 broadcast_multiply_fusion
  27.6 0.7 broadcast_compare_fusion
  28.3 0.1 copy.35
  28.5 0.7 convert_element_type.46
  29.2 0.1 copy.41
  29.4 0.1 broadcast_add_fusion
  29.7 7.6 %scatter_custom_fusion = bf16[512]{0:T(512)(128)(2,1)S(1)} fusion(s32[1024]{0:T(1024)S(1)} %bitcast.70, bf16[1024]{0:T(1024)(128)(2,1)S(1)} %reshape.171, bf16[]{:T(256)} %constant.43.clone.1), kind=kCustom, calls=%fused_computation.45 | custom fusion | bytes 1026 | tf_op jit(solution)/shard_map/scatter | solution.py:28
  37.2 0.7 all_to_all.12
  38.0 19.1 %all-to-all-start = ((bf16[64,1,8]{2,1,0:T(2,128)(2,1)}), bf16[64,1,8]{2,1,0:T(2,128)(2,1)S(1)}, u32[]{:S(2)}, u32[]{:S(2)}) async-start(bf16[64,1,8]{2,1,0:T(2,128)(2,1)} %all_to_all.12), calls=%async_computation | async-start | bytes 65536 | tf_op jit(solution)/shard_map/all_to_all | solution.py:54
  57.1 4.5 %scatter_custom_fusion.1 = s32[512]{0:T(512)S(1)} fusion(s32[1024]{0:T(1024)S(1)} %bitcast.71, s32[1024]{0:T(1024)S(1)} %add_select_fusion, s32[]{:T(128)} %constant.48.clone.1), kind=kCustom, calls=%fused_computation.42 | custom fusion | bytes 2052 | tf_op jit(solution)/shard_map/scatter | solution.py:24
  61.8 15.6 %gather_fusion = bf16[512,7168]{1,0:T(8,128)(2,1)} fusion(bf16[128,7168]{1,0:T(8,128)(2,1)} %all-gather.2.cloned.1.call-done, s32[1024]{0:T(1024)S(1)} %pad_clamp_fusion), kind=kCustom, calls=%fused_computation | custom fusion | bytes 14682112 | tf_op jit(solution)/shard_map/jit(_take)/gather | solution.py:50
  77.5 7.0 %fusion.2 = bf16[64,8,7168]{2,1,0:T(8,128)(2,1)} fusion(bf16[512,7168]{1,0:T(8,128)(2,1)} %gather_fusion, pred[64,8]{1,0:T(8,128)(4,1)S(1)} %broadcast_in_dim.56, pred[64,8]{1,0:T(8,128)(4,1)S(1)} %broadcast_in_dim.54), kind=kLoop, calls=%fused_computation.6 | loop fusion | flops 7340032 | bytes 14681088 | tf_op jit(solution)/shard_map/jit(_where)/select_n | solution.py:49
  84.4 15.1 %all-to-all-start.1 = ((bf16[64,8,7168]{2,1,0:T(8,128)(2,1)}), bf16[64,8,7168]{2,1,0:T(8,128)(2,1)}, u32[]{:S(2)}, u32[]{:S(2)}) async-start(bf16[64,8,7168]{2,1,0:T(8,128)(2,1)} %fusion.2), calls=%async_computation.1 | async-start | bytes 14680064 | tf_op jit(solution)/shard_map/all_to_all | solution.py:53
  99.6 6.0 %copy.43 = bf16[1,2,7168,128]{2,3,1,0:T(8,128)(2,1)} copy(bf16[1,2,7168,128]{3,2,1,0:T(8,128)(2,1)} %param.8) | data formatting | bytes 7340032 | tf_op args[3]
  105.6 0.1 broadcast_in_dim.51
  105.7 0.1 convert_element_type.51
  105.8 4.1 bitcast_multiply_fusion
  110.1 306.8 %all-to-all-done.1 = bf16[64,8,7168]{2,1,0:T(8,128)(2,1)} async-done(((bf16[64,8,7168]{2,1,0:T(8,128)(2,1)}), bf16[64,8,7168]{2,1,0:T(8,128)(2,1)}, u32[]{:S(2)}, u32[]{:S(2)}) %all-to-all-start.1) | async-done | bytes 7340064 | tf_op jit(solution)/shard_map/all_to_all | solution.py:53
  416.9 10.2 %fusion.5 = f32[2,64,8,128]{3,1,2,0:T(8,128)S(1)} fusion(bf16[64,8,7168]{2,1,0:T(8,128)(2,1)} %all-to-all-done.1, bf16[2,7168,128]{1,2,0:T(8,128)(2,1)} %bitcast_multiply_fusion), kind=kOutput, calls=%fused_computation.10 | convolution fusion | flops 1879048192 | bytes 11534336 | tf_op jit(solution)/shard_map/scd,kdf->kscf/dot_general | solution.py:55
  427.2 1.0 fusion.13
  (28 shorter events, 1.4 us)
Async XLA Ops:
  6.5 55.3 %all-gather.2.cloned.1.call-start = ((), (), s32[]{:S(2)}) async-start(), calls=%async_computation.2 | async-start | bytes 2064384 | tf_op jit(solution)/shard_map/all_gather | solution.py:48
  38.0 46.5 %all-to-all-start = ((bf16[64,1,8]{2,1,0:T(2,128)(2,1)}), bf16[64,1,8]{2,1,0:T(2,128)(2,1)S(1)}, u32[]{:S(2)}, u32[]{:S(2)}) async-start(bf16[64,1,8]{2,1,0:T(2,128)(2,1)} %all_to_all.12), calls=%async_computation | async-start | bytes 65536 | tf_op jit(solution)/shard_map/all_to_all | solution.py:54
  84.4 21.1 %copy-start = (s32[1,2,112,2]{2,3,1,0:T(2,128)S(1)}, s32[1,2,112,2]{2,3,1,0:T(2,128)}, u32[]{:S(2)}) copy-start(s32[1,2,112,2]{2,3,1,0:T(2,128)} %param.9) | copy-start | bytes 5380
  84.4 332.4 %all-to-all-start.1 = ((bf16[64,8,7168]{2,1,0:T(8,128)(2,1)}), bf16[64,8,7168]{2,1,0:T(8,128)(2,1)}, u32[]{:S(2)}, u32[]{:S(2)}) async-start(bf16[64,8,7168]{2,1,0:T(8,128)(2,1)} %fusion.2), calls=%async_computation.1 | async-start | bytes 14680064 | tf_op jit(solution)/shard_map/all_to_all | solution.py:53
Sparse Core Ops, SparseCore 0:
  9.5 38.3 all-gather.1
where the time goes:
time: 442 us; the launch traced here: 435 us
  waiting for transfers between devices  307 us (69%)
  local copies, waits for them, and re-layouts  37 us (8%)
  starting transfers between devices  34.2 us (8%)
  other arithmetic  32.5 us (7%)
  between operations  13.6 us (3%)
  matrix products  10.2 us (2%)
    all_to_all x1, waiting for transfers between devices, shards(): lax.all_to_all(outgoing, 'expert', split_axis=0, concat_axis=0, tiled=True)  307 us
    all_to_all x1, starting transfers between devices, shards(): lax.all_to_all(slot_weight, 'expert', split_axis=0, concat_axis=0, tiled=...  19.1 us
    another operation x3, other arithmetic  18.2 us
    gather x1, local copies, waits for them, and re-layouts, shards(): jnp.take(gathered, clipped, axis=0)  15.6 us
    all_to_all x1, starting transfers between devices, shards(): lax.all_to_all(outgoing, 'expert', split_axis=0, concat_axis=0, tiled=True)  15.1 us
    dot_general x1, matrix products, shards(): jnp.einsum('scd,kdf->kscf', arrived, masked, preferred_element_type=jnp.f...  10.2 us
  transfers between devices with their start and end apart: 3, of which 1 were waited for; matrix products, arithmetic and copies ran while one was open for 16% of the time, Pallas kernels for 0%

commit v1 on v0

v1 whole, which is shorter than its diff:
```python
import functools

import jax
import jax.numpy as jnp
from jax import lax
from jax.experimental import pallas as pl
from jax.experimental.pallas import tpu as pltpu
from jax.sharding import PartitionSpec as P

BLOCK = 64
CAP = 8
MESH = pl.DeviceIdType.MESH
ZS, XS, YS, CS = 16, 4, 4, 2
HALF = 64


def kernel(dims, tok_ref, ids_ref, rw_ref, keep_ref, gu_ref, out_ref,
           zb, mb, xs, ws, wr, act, wraw, wm, maskv, res,
           z_s, z_r, m_s, m_r, x_s, x_r, w_s, w_r,
           y_s, y_r, h_s, h_r, c_s, c_r, l_sem):
    Z, X, Y, C = dims
    U = Z // 2
    T, F = tok_ref.shape
    D = F * Y * C
    H = out_ref.shape[1]
    NB = D // BLOCK
    XH = X // 2
    f32, bf16 = jnp.float32, jnp.bfloat16

    e = lax.axis_index("expert")
    t = lax.axis_index("tensor")
    z, x = e // X, e % X
    y, c = t // C, t % C
    up, down = ((z + 1) % Z) * X + x, ((z + Z - 1) % Z) * X + x
    z_to = (up, down)
    yn, yp, yo = (y + 1) % Y, (y + Y - 1) % Y, (y + 2) % Y
    y_to = (yn * C + c, yp * C + c)
    sib = y * C + 1 - c

    def cols(yy, cc):
        return pl.ds(pl.multiple_of((yy * C + cc) * F, 128), F)

    barrier = pltpu.get_barrier_semaphore()
    partners = [(up, t), (down, t), (e, y_to[0]), (e, y_to[1]), (e, sib)]
    partners += [(z * X + (x + k) % X, t) for k in range(1, X)]
    for dev in partners:
        pl.semaphore_signal(barrier, inc=1, device_id=dev, device_id_type=MESH)
    w_copy = pltpu.make_async_copy(gu_ref, wraw, l_sem.at[0])
    w_copy.start()
    own_copy = pltpu.make_async_copy(tok_ref, zb.at[U - 1, 1], l_sem.at[1])
    own_copy.start()
    pl.semaphore_wait(barrier, len(partners))

    TH = T // 2

    def z_copy(src, unit, d, h, slot):
        return pltpu.make_async_remote_copy(
            src_ref=src, dst_ref=zb.at[unit, slot, pl.ds(h * TH, TH)],
            send_sem=z_s.at[unit, d, h], recv_sem=z_r.at[unit, d, h],
            device_id=(z_to[d], t), device_id_type=MESH)

    def m_copy(src, unit, d, slot):
        return pltpu.make_async_remote_copy(
            src_ref=src, dst_ref=mb.at[unit, slot],
            send_sem=m_s.at[unit, d], recv_sem=m_r.at[unit, d],
            device_id=(z_to[d], t), device_id_type=MESH)

    for h in range(2):
        for d in range(2):
            z_copy(tok_ref.at[pl.ds(h * TH, TH)], 0, d, h, d).start()

    lane = lax.broadcasted_iota(jnp.int32, (T, 128), 1)
    row = lax.broadcasted_iota(jnp.int32, (T, 128), 0)
    lane_e = lane % HALF
    ids = ids_ref[...]
    rw = rw_ref[...].astype(bf16).astype(f32)
    hit = jnp.zeros((T, 128), f32)
    val = jnp.zeros((T, 128), f32)
    for k in range(ids.shape[1]):
        eq = ids[:, k:k + 1] == lane_e
        hit = jnp.where(eq, 1.0, hit)
        val = jnp.where(eq, rw[:, k:k + 1], val)
    tri = (lax.broadcasted_iota(jnp.int32, (T, T), 1)
           < lax.broadcasted_iota(jnp.int32, (T, T), 0))
    rank = jnp.dot(tri.astype(f32).astype(bf16), hit.astype(bf16), preferred_element_type=f32)
    rank = jnp.where(hit > 0.5, rank, -1.0)
    val = jnp.where(lane < HALF, (row + 1).astype(f32), val)
    sub8 = lax.broadcasted_iota(jnp.int32, (CAP, 128), 0)
    lane8 = lax.broadcasted_iota(jnp.int32, (CAP, 128), 1)
    meta = jnp.zeros((CAP, 128), f32)
    for k in range(CAP):
        total = jnp.sum(jnp.where(rank == float(k), val, 0.0), axis=0, keepdims=True)
        meta = jnp.where(sub8 == k, total, meta)
    mb[U - 1, 1] = meta

    keep = keep_ref[...].astype(f32)
    klane = lax.broadcasted_iota(jnp.int32, (2 * NB, 128), 1)
    maskv[...] = jnp.where(klane < BLOCK, keep[:, 0:1], keep[:, 1:2])
    for d in range(2):
        m_copy(mb.at[U - 1, 1], 0, d, d).start()

    w_copy.wait()

    def mask_block(b, carry):
        start = pl.multiple_of(b * BLOCK, BLOCK)
        for k in range(2):
            line = maskv[pl.ds(k * NB + b, 1), :].astype(bf16)
            wm[pl.ds(start, BLOCK), k * H:(k + 1) * H] = wraw[k, pl.ds(start, BLOCK), :] * line
        return carry

    lax.fori_loop(0, NB, mask_block, 0)
    own_copy.wait()

    def x_copies(u, k):
        to = (x + k) % X
        dev = (z * X + to, t)
        return (
            pltpu.make_async_remote_copy(
                src_ref=xs.at[u, to], dst_ref=act.at[u, x, :, cols(y, c)],
                send_sem=x_s.at[u, k - 1], recv_sem=x_r.at[u, k - 1],
                device_id=dev, device_id_type=MESH),
            pltpu.make_async_remote_copy(
                src_ref=ws.at[u, to], dst_ref=wr.at[u, x],
                send_sem=w_s.at[u, k - 1], recv_sem=w_r.at[u, k - 1],
                device_id=dev, device_id_type=MESH))

    def x_local(u):
        return (pltpu.make_async_copy(xs.at[u, x], act.at[u, x, :, cols(y, c)], l_sem.at[2 + u]),
                pltpu.make_async_copy(ws.at[u, x], wr.at[u, x], l_sem.at[2 + U + u]))

    def x_wait_recv(u, k):
        frm = (x + X - k) % X
        dev = (z * X + frm, t)
        for src, dst, s, r in ((xs.at[u, frm], act.at[u, frm, :, cols(y, c)], x_s, x_r),
                               (ws.at[u, frm], wr.at[u, frm], w_s, w_r)):
            pltpu.make_async_remote_copy(
                src_ref=src, dst_ref=dst, send_sem=s.at[u, k - 1], recv_sem=r.at[u, k - 1],
                device_id=dev, device_id_type=MESH).wait_recv()

    def y_copy(u, d, yy):
        ref = act.at[u, :, :, cols(yy, c)]
        return pltpu.make_async_remote_copy(
            src_ref=ref, dst_ref=ref, send_sem=y_s.at[u, d], recv_sem=y_r.at[u, d],
            device_id=(e, y_to[d]), device_id_type=MESH)

    def h_copy(u, d, yy):
        ref = act.at[u, pl.ds(d * XH, XH), :, cols(yy, c)]
        return pltpu.make_async_remote_copy(
            src_ref=ref, dst_ref=ref, send_sem=h_s.at[u, d], recv_sem=h_r.at[u, d],
            device_id=(e, y_to[d]), device_id_type=MESH)

    def c_copy(u, j, yy, cc):
        ref = act.at[u, :, :, cols(yy, cc)]
        return pltpu.make_async_remote_copy(
            src_ref=ref, dst_ref=ref, send_sem=c_s.at[u, j], recv_sem=c_r.at[u, j],
            device_id=(e, sib), device_id_type=MESH)

    def select(u):
        zero = jnp.zeros((CAP, T), f32)
        hots, weights = [], []
        for xx in range(X):
            for d in range(2):
                m = mb[u, d]
                want = z * X + xx
                tok = jnp.sum(jnp.where(lane8 == want, m, 0.0), axis=1, keepdims=True)
                wgt = jnp.sum(jnp.where(lane8 == want + HALF, m, 0.0), axis=1, keepdims=True)
                hot = jnp.where(tok == (lane8 + 1).astype(f32), 1.0, 0.0)
                hots.append(jnp.concatenate([hot, zero] if d == 0 else [zero, hot], axis=1))
                weights.append(jnp.broadcast_to(wgt, (CAP, 128)))
        hot = jnp.concatenate(hots, axis=0).astype(bf16)
        picked = jnp.dot(hot, zb[u].reshape(2 * T, F), preferred_element_type=f32)
        xs[u] = picked.astype(bf16).reshape(X, 2 * CAP, F)
        ws[u] = jnp.concatenate(weights, axis=0).astype(bf16).reshape(X, 2 * CAP, 128)

    def multiply(u):
        acc = jnp.dot(act[u].reshape(X * 2 * CAP, D), wm[...], preferred_element_type=f32)
        gate, upp = acc[:, :H], acc[:, H:]
        scale = wr[u].reshape(X * 2 * CAP, 128).astype(f32)
        hid = scale * (gate / (1.0 + jnp.exp(-gate))) * upp
        near, far = (z + Z - (u + 1)) % Z, (z + (u + 1) % U) % Z
        for xx in range(X):
            for d in range(2):
                s = (near if d == 0 else far) * X + xx
                r = (xx * 2 + d) * CAP
                res[pl.ds(pl.multiple_of(s * CAP, CAP), CAP), :] = hid[r:r + CAP]

    def step(i, carry):
        @pl.when(i < U - 1)
        def _():
            for d in range(2):
                z_copy(zb.at[i, d, pl.ds(0, TH)], i, d, 0, d).wait_recv()

                @pl.when(i < U - 2)
                def _():
                    z_copy(zb.at[i, d, pl.ds(0, TH)], i + 1, d, 0, d).start()
            for d in range(2):
                m_copy(mb.at[i, d], i, d, d).wait_recv()

                @pl.when(i < U - 2)
                def _():
                    m_copy(mb.at[i, d], i + 1, d, d).start()

        @pl.when(i == U - 2)
        def _():
            z_copy(zb.at[U - 2, 0, pl.ds(0, TH)], U - 1, 0, 0, 0).start()
            m_copy(mb.at[U - 2, 0], U - 1, 0, 0).start()

        @pl.when((i >= 1) & (i < U + 1))
        def _():
            u = i - 1
            for copy in x_local(u):
                copy.wait()
            for k in range(1, X):
                x_wait_recv(u, k)
            for d in range(2):
                y_copy(u, d, y).start()
            c_copy(u, 0, y, c).start()

        @pl.when((i >= 2) & (i < U + 2))
        def _():
            u = i - 2
            for d in range(2):
                yy = yp if d == 0 else yn
                y_copy(u, d, yy).wait_recv()
                h_copy(u, d, yy).start()
                c_copy(u, 1 + d, yy, c).start()

        @pl.when((i >= 3) & (i < U + 3))
        def _():
            u = i - 3
            for d in range(2):
                h_copy(u, d, yo).wait_recv()
            c_copy(u, 3, yo, c).start()

        @pl.when(i < U - 1)
        def _():
            for d in range(2):
                z_copy(zb.at[i, d, pl.ds(TH, TH)], i, d, 1, d).wait_recv()

                @pl.when(i < U - 2)
                def _():
                    z_copy(zb.at[i, d, pl.ds(TH, TH)], i + 1, d, 1, d).start()

        @pl.when(i == U - 2)
        def _():
            z_copy(zb.at[U - 2, 1, pl.ds(TH, TH)], U - 1, 1, 1, 0).start()

        @pl.when(i == U - 1)
        def _():
            z_copy(zb.at[U - 1, 0, pl.ds(0, TH)], U - 1, 0, 0, 0).wait_recv()
            m_copy(mb.at[U - 1, 0], U - 1, 0, 0).wait_recv()
            z_copy(zb.at[U - 1, 0, pl.ds(TH, TH)], U - 1, 1, 1, 0).wait_recv()

        @pl.when(i < U)
        def _():
            select(i)
            for k in range(1, X):
                for copy in x_copies(i, k):
                    copy.start()
            for copy in x_local(i):
                copy.start()

        @pl.when(i >= 4)
        def _():
            u = i - 4
            for j, yy in enumerate((y, yp, yn, yo)):
                c_copy(u, j, yy, 1 - c).wait_recv()
            multiply(u)

        return carry

    lax.fori_loop(0, U + 4, step, 0)

    def drain(u, carry):
        @pl.when(u < U - 1)
        def _():
            for d in range(2):
                m_copy(mb.at[u, d], u, d, d).wait_send()
                for h in range(2):
                    z_copy(zb.at[u, d, pl.ds(h * TH, TH)], u, d, h, d).wait_send()
        for k in range(1, X):
            for copy in x_copies(u, k):
                copy.wait_send()
        for d in range(2):
            y_copy(u, d, y).wait_send()
            h_copy(u, d, yo).wait_send()
        for j in range(4):
            c_copy(u, j, y, c).wait_send()
        return carry

    lax.fori_loop(0, U, drain, 0)
    z_copy(zb.at[U - 1, 0, pl.ds(0, TH)], U - 1, 0, 0, 0).wait_send()
    z_copy(zb.at[U - 1, 0, pl.ds(TH, TH)], U - 1, 1, 1, 0).wait_send()
    m_copy(mb.at[U - 1, 0], U - 1, 0, 0).wait_send()
    out_ref[...] = res[...].astype(out_ref.dtype)


def shards(dims, tokens, route_ids, route_weight, gate_up, block_keep):
    Z, X, Y, C = dims
    U = Z // 2
    T, F = tokens.shape
    D = F * Y * C
    H = gate_up.shape[3]
    NB = D // BLOCK
    bf16, f32 = jnp.bfloat16, jnp.float32
    dma = pltpu.SemaphoreType.DMA
    vmem = pl.BlockSpec(memory_space=pltpu.VMEM)
    hbm = pl.BlockSpec(memory_space=pl.ANY)
    out = pl.pallas_call(
        functools.partial(kernel, dims),
        out_shape=jax.ShapeDtypeStruct((Z * X * CAP, H), bf16),
        in_specs=[hbm, vmem, vmem, vmem, hbm],
        out_specs=vmem,
        scratch_shapes=[
            pltpu.VMEM((U, 2, T, F), bf16),
            pltpu.VMEM((U, 2, CAP, 128), f32),
            pltpu.VMEM((U, X, 2 * CAP, F), bf16),
            pltpu.VMEM((U, X, 2 * CAP, 128), bf16),
            pltpu.VMEM((U, X, 2 * CAP, 128), bf16),
            pltpu.VMEM((U, X, 2 * CAP, D), bf16),
            pltpu.VMEM((2, D, H), bf16),
            pltpu.VMEM((D, 2 * H), bf16),
            pltpu.VMEM((2 * NB, 128), f32),
            pltpu.VMEM((Z * X * CAP, H), f32),
            dma((U, 2, 2)), dma((U, 2, 2)),
            dma((U, 2)), dma((U, 2)),
            dma((U, X - 1)), dma((U, X - 1)),
            dma((U, X - 1)), dma((U, X - 1)),
            dma((U, 2)), dma((U, 2)),
            dma((U, 2)), dma((U, 2)),
            dma((U, 4)), dma((U, 4)),
            dma((2 + 2 * U,)),
        ],
        compiler_params=pltpu.CompilerParams(
            collective_id=0, has_side_effects=True, vmem_limit_bytes=56 * 1024 * 1024),
    )(tokens, route_ids, route_weight, block_keep.reshape(2 * NB, H // BLOCK), gate_up[0])
    return out.reshape(1, Z * X * CAP, H)


def build(mesh, dims):
    return jax.shard_map(
        functools.partial(shards, dims),
        mesh=mesh,
        in_specs=(
            P("expert", "tensor"),
            P("expert", None),
            P("expert", None),
            P("expert", None, None, "tensor"),
            P("expert", None, None, "tensor"),
        ),
        out_specs=P("expert", None, "tensor"),
        check_vma=False,
    )


def solution(mesh):
    return build(mesh, (ZS, XS, YS, CS))
```

time: 442 us -> 83.2 us (0.19); the launches traced: 435 us -> 82.9 us
  waiting for transfers between devices: 307 us -> 0 us
  Pallas kernels: 0 us -> 77.1 us
  starting transfers between devices: 34.2 us -> 0 us
  other arithmetic: 32.5 us -> 0 us
  local copies, waits for them, and re-layouts: 37 us -> 5.83 us
  between operations: 13.6 us -> 0.01 us
  matrix products: 10.2 us -> 0 us
    all_to_all x2 -> x0, waiting for transfers between devices: 307 us -> none  [the longest x1 307 us: shards(): lax.all_to_all(outgoing, 'expert', split_axis=0, concat_axis=0, tiled=True)]
    pallas_call x0 -> x1, Pallas kernels: none -> 77.1 us  [shards(): pl.pallas_call(functools.partial(kernel, dims), out_shape=jax.ShapeDtypeS...]
    all_to_all x2 -> x0, starting transfers between devices: 34.2 us -> none  [the longest x1 19.1 us: shards(): lax.all_to_all(slot_weight, 'expert', split_axis=0, concat_axis=0, tiled=...]
    another operation x3 -> x0, other arithmetic: 18.2 us -> none
    gather x1 -> x0, local copies, waits for them, and re-layouts: 15.6 us -> none  [shards(): jnp.take(gathered, clipped, axis=0)]
    scatter x2 -> x0, local copies, waits for them, and re-layouts: 12.1 us -> none  [the longest x1 7.58 us: slot_table(): weight_of = jnp.zeros((flight * capacity,), rounded.dtype).at[target].set...]
    dot_general x1 -> x0, matrix products: 10.2 us -> none  [shards(): jnp.einsum('scd,kdf->kscf', arrived, masked, preferred_element_type=jnp.f...]
    select_n x3 -> x0, other arithmetic: 6.99 us -> none  [the longest x1 6.97 us: shards(): jnp.where(filled, jnp.take(gathered, clipped, axis=0), jnp.zeros((), gath...]
  transfers between devices with their start and end apart: 3 -> 0, of which waited for: 1 -> 0; matrix products, arithmetic and copies ran while one was open for 16% -> 0% of each run, Pallas kernels for 0% -> 0%
where the time goes in v1:
time: 83.2 us; the launch traced here: 82.9 us
  Pallas kernels  77.1 us (93%)
  local copies, waits for them, and re-layouts  5.83 us (7%)
    pallas_call x1, Pallas kernels, shards(): pl.pallas_call(functools.partial(kernel, dims), out_shape=jax.ShapeDtypeS...  77.1 us
    unnamed x4, local copies, waits for them, and re-layouts  5.83 us

profile of v1, /device:TPU:1, one launch (start us, length us, event | category | flops | bytes accessed | tf_op | source)
XLA Modules:
  0.0 82.9 jit_solution(1504474422367586736)
XLA Ops:
  0.0 1.4 %copy.7.ids_ref = s32[128,8]{1,0:T(8,128)} copy(s32[128,8]{0,1:T(8,128)} %param.6) | data formatting | bytes 8192 | tf_op args[1]
  1.4 1.4 %copy.8.rw_ref = f32[128,8]{1,0:T(8,128)} copy(f32[128,8]{0,1:T(8,128)} %param.7) | data formatting | bytes 8192 | tf_op args[2]
  2.8 1.5 %copy.6 = s32[1,2,112,2]{3,2,1,0:T(8,128)} copy(s32[1,2,112,2]{2,3,1,0:T(2,128)} %param.9) | data formatting | bytes 3584 | tf_op args[4]
  4.3 77.1 %shard_map.55 = bf16[512,128]{1,0:T(8,128)(2,1)} custom-call(bf16[128,896]{1,0:T(8,128)(2,1)} %tok_ref.1, s32[128,8]{1,0:T(8,128)} %copy.7.ids_ref, f32[128,8]{1,0:T(8,128)} %copy.8.rw_ref, s32[224,2]{1,0:T(8,128)} %bitcast.5, bf16[2,7168,128]{2,1,0:T(8,128)(2,1)} %bitcast.3), custom_call_target="tpu_custom_call" | custom-call | tf_op jit(solution)/shard_map/pallas_call | solution.py:309
  81.4 1.6 %copy.10 = bf16[1,512,128]{2,1,0:T(8,128)(2,1)} copy(bf16[1,512,128]{2,1,0:T(8,128)(2,1)} %bitcast.4) | data formatting | bytes 262144
